TPU v7x, 256 devices: a whole 4x4x8 slice. The times are simulated.
256 devices in a mesh: tile: 64 (over z, x, core), mem: 4 (over y).
Axes of the slice: x: 4, y: 4, z: 8, core: 2. Of those that a mesh axis runs over, the one named last changes fastest.
Arguments:
- footprints: bfloat16 [8192, 128, 128], P('tile'), may hold values from -0.1875 to 0.1875
- tile_row: int32 [8192], P('tile'), may hold values from 0 to 1023, as said below
- tile_col: int32 [8192], P('tile'), may hold values from 0 to 511, as said below
- prior_flux: bfloat16 [256, 65536], P('mem', 'tile'), may hold values from -12 to 12
- observed: float32 [256, 131072], P('mem', 'tile'), may hold values from -6 to 6
- precision_weight: int32 [131072], P('tile'), may hold values from 1 to 16
Outputs:
- gradient: float32 [256, 65536], P('mem', 'tile')
Inputs may be any that keep to these rules, and one draw needn't show every extreme that they name: Among the 128 tiles of each index of tile, at most 3 have a row block of one owner (owner = tile_row // 16); in every draw one owner gets exactly 3 from every index. Likewise with owner = tile_col // 8: at most 3 from one index of tile to one owner, and one owner gets exactly 3 from every index.
All inputs are finite; a program needn't handle non-finite values.
Results may differ from a plain program's by a relative error of at most 0.0052.
Values may be sent and summed in bfloat16 or wider, within the bound.
A program may use at most 64 MiB of HBM per device.

v0:
```python
import jax
import jax.numpy as jnp
from jax import lax
from jax.sharding import PartitionSpec as P

MEMBERS = 256
FLUX_DEV = 8
SOUND_DEV = 16


def sent_to_all(value, axis):
    size = lax.axis_size(axis)
    return lax.all_to_all(
        jnp.broadcast_to(value[None], (size, *value.shape)), axis, 0, 0, tiled=True
    )


def over_copies(value, axis):
    return sent_to_all(value, axis).sum(axis=0)


def slot_of(owners, capacity):
    entries = owners.shape[0]
    position = jnp.arange(entries)
    earlier = (owners[:, None] == owners[None, :]) & (position[None, :] < position[:, None])
    return owners * capacity + jnp.sum(earlier.astype(jnp.int32), axis=1)


def invert(slot_ids, slot_total):
    matches = slot_ids[None, :] == jnp.arange(slot_total)[:, None]
    sources = jnp.sum(jnp.where(matches, jnp.arange(slot_ids.shape[0])[None, :], 0), axis=1)
    return (sources, jnp.any(matches, axis=1))


def to_slots(values, sources, usage_flags):
    placed = jnp.take(values, sources, axis=1)
    return jnp.where(usage_flags[None, :, None], placed, jnp.zeros_like(placed))


def body(footprints, tile_row, tile_col, prior_flux, observed, precision_weight):
    devices_tile = lax.axis_size("tile")
    tile_count = footprints.shape[0]
    tile_size = footprints.shape[1]
    capacity = tile_count // devices_tile + max(1, tile_count // (2 * devices_tile))
    slot_total = devices_tile * capacity
    local_members = prior_flux.shape[0]
    local_sum = jnp.sum(prior_flux.astype(jnp.float32), axis=0)
    ensemble_sum = over_copies(local_sum, "mem")
    ensemble_mean = ensemble_sum / MEMBERS
    member_deviations = (prior_flux.astype(jnp.float32) - ensemble_mean[None, :]).astype(
        jnp.bfloat16
    )
    row_owner = tile_row // SOUND_DEV
    row_local = tile_row % SOUND_DEV
    col_owner = tile_col // FLUX_DEV
    col_local = tile_col % FLUX_DEV
    row_slot = slot_of(row_owner, capacity)
    col_slot = slot_of(col_owner, capacity)
    row_source, row_used = invert(row_slot, slot_total)
    col_source, col_used = invert(col_slot, slot_total)
    gathered = lax.all_gather(member_deviations, "tile", axis=1, tiled=True)
    retrieved_blocks = jnp.take(gathered.reshape(local_members, -1, tile_size), tile_col, axis=1)
    forward_terms = jnp.einsum(
        "mtk,trk->mtr", retrieved_blocks, footprints, preferred_element_type=jnp.float32
    )
    row_index = jnp.where(row_used, jnp.take(row_local, row_source), SOUND_DEV)
    sent_terms = to_slots(forward_terms, row_source, row_used)
    got_terms, got_rows = (
        lax.all_to_all(
            sent_terms.astype(jnp.bfloat16), "tile", split_axis=1, concat_axis=1, tiled=True
        ).astype(sent_terms.dtype),
        lax.all_to_all(row_index[None, :], "tile", split_axis=1, concat_axis=1, tiled=True),
    )
    got_rows = got_rows[0]
    row_match = (got_rows[None, :] == jnp.arange(SOUND_DEV)[:, None]).astype(jnp.float32)
    modelled = jnp.einsum("ds,msk->mdk", row_match, got_terms, precision=lax.Precision.HIGHEST)
    targets = observed.reshape(local_members, SOUND_DEV, tile_size)
    obs_weight = (precision_weight.astype(jnp.float32) / 8.0).reshape(SOUND_DEV, tile_size)
    weighted = (obs_weight[None, :, :] * (modelled - targets)).astype(jnp.bfloat16)
    reply_rows = jnp.take(weighted, jnp.minimum(got_rows, SOUND_DEV - 1), axis=1)
    returned = lax.all_to_all(reply_rows, "tile", split_axis=1, concat_axis=1, tiled=True)
    residual_tiles = jnp.take(returned, row_slot, axis=1)
    backward_terms = jnp.einsum(
        "mtr,trk->mtk", residual_tiles, footprints, preferred_element_type=jnp.float32
    )
    col_index = jnp.where(col_used, jnp.take(col_local, col_source), FLUX_DEV)
    sent_back = to_slots(backward_terms, col_source, col_used)
    got_back, got_cols = (
        lax.all_to_all(
            sent_back.astype(jnp.bfloat16), "tile", split_axis=1, concat_axis=1, tiled=True
        ).astype(sent_back.dtype),
        lax.all_to_all(col_index[None, :], "tile", split_axis=1, concat_axis=1, tiled=True),
    )
    col_match = (got_cols[0][None, :] == jnp.arange(FLUX_DEV)[:, None]).astype(jnp.float32)
    reduced_total = jnp.einsum("fs,msk->mfk", col_match, got_back, precision=lax.Precision.HIGHEST)
    gradient = reduced_total.reshape(local_members, FLUX_DEV * tile_size)
    return gradient


def solution(mesh):
    in_specs = (
        P("tile", None, None),
        P("tile"),
        P("tile"),
        P("mem", "tile"),
        P("mem", "tile"),
        P("tile"),
    )
    out_specs = P("mem", "tile")
    return jax.shard_map(body, mesh=mesh, in_specs=in_specs, out_specs=out_specs, check_vma=False)
```

profile of v0, /device:TPU:2, one launch (start us, length us, event | category | flops | bytes accessed | tf_op | source)
XLA Modules:
  0.0 407.8 jit_solution(12967651325447050244)
XLA Ops:
  6.5 0.0 all-gather.2.cloned.1.call-start
  6.5 0.9 convert_reduce_fusion
  7.5 9.6 %all_to_all.39 = f32[4,1,1024]{2,1,0:T(1,128)S(1)} all-to-all(f32[4,1,1024]{2,1,0:T(1,128)S(1)} %broadcast_in_dim.122), channel_id=1, replica_groups=mesh['tile'=64,'mem'=4] {'mem'}, dimensions={0} | all-to-all | bytes 32768 | tf_op jit(solution)/shard_map/all_to_all | solution.py:13
  17.2 1.6 fusion.26
  18.7 0.0 all-gather.2.cloned.1.call-update
  18.8 0.7 and_select_fusion.1
  19.4 0.2 convert_reduce_fusion.1
  19.6 0.1 select_reduce_fusion.1
  19.8 1.6 gather_fusion.3
  21.3 0.1 fusion.27
  21.5 0.7 all_to_all.25
  22.2 12.0 %all-to-all-start = ((s32[1,64,3]{2,0,1:T(1,128)}), s32[1,64,3]{2,0,1:T(1,128)S(1)}, u32[]{:S(2)}, u32[]{:S(2)}) async-start(s32[1,64,3]{2,0,1:T(1,128)} %bitcast), calls=%async_computation | async-start | bytes 65536 | tf_op jit(solution)/shard_map/all_to_all | solution.py:72
  34.2 0.7 and_select_fusion
  34.9 0.7 compare_and_fusion.2
  35.6 66.0 %all-gather.2.cloned.1.call-done = bf16[64,65536]{1,0:T(8,128)(2,1)} async-done(((bf16[64,1024]{1,0:T(8,128)(2,1)}), bf16[64,65536]{1,0:T(8,128)(2,1)}) %all-gather.2.cloned.1.call-update) | async-done | bytes 8388624 | tf_op jit(solution)/shard_map/all_gather | solution.py:61
  101.5 9.0 %copy_bitcast_fusion = bf16[64,512,128]{2,0,1:T(8,128)(2,1)} fusion(bf16[64,65536]{1,0:T(8,128)(2,1)} %all-gather.2.cloned.1.call-done), kind=kLoop, calls=%fused_computation.7 | loop fusion | bytes 16777216 | tf_op jit(solution)/shard_map/reshape | solution.py:62
  110.5 5.5 %gather_fusion = bf16[128,64,128]{2,1,0:T(8,128)(2,1)} fusion(bf16[64,512,128]{2,0,1:T(8,128)(2,1)} %copy_bitcast_fusion, s32[1024]{0:T(1024)S(1)} %pad_clamp_fusion.3), kind=kCustom, calls=%fused_computation.4 | custom fusion | bytes 4194816 | tf_op jit(solution)/shard_map/jit(_take)/gather | solution.py:62
  116.1 5.8 %convolution_bitcast_fusion.1 = bf16[64,128,128]{2,0,1:T(8,128)(2,1)S(1)} fusion(bf16[128,128,128]{2,1,0:T(8,128)(2,1)} %param.10, bf16[128,64,128]{2,1,0:T(8,128)(2,1)} %gather_fusion, pred[128]{0:T(512)(128)(4,1)S(1)} %compare_and_fusion.2), kind=kOutput, calls=%fused_computation.18 | convolution fusion | flops 269484032 | bytes 8388736 | tf_op jit(solution)/shard_map/mtk,trk->mtr/dot_general | solution.py:63
  121.8 2.7 gather_fusion.4
  124.6 4.3 %fusion.1 = bf16[64,192,128]{2,0,1:T(8,128)(2,1)} fusion(bf16[192,64,128]{2,1,0:T(8,128)(2,1)} %gather_fusion.4, pred[192]{0:T(512)(128)(4,1)S(1)} %get-tuple-element.14, pred[192]{0:T(512)(128)(4,1)S(1)} %fusion.27), kind=kLoop, calls=%fused_computation.11 | loop fusion | flops 3145728 | bytes 6291840 | tf_op jit(solution)/shard_map/convert_element_type | solution.py:70
  128.8 0.0 copy-start
  128.8 0.0 all-to-all-done
  128.8 7.8 %all-to-all-start.2 = ((bf16[64,192,128]{2,0,1:T(8,128)(2,1)}), bf16[64,192,128]{2,0,1:T(8,128)(2,1)S(1)}, u32[]{:S(2)}, u32[]{:S(2)}) async-start(bf16[64,192,128]{2,0,1:T(8,128)(2,1)} %fusion.1), calls=%async_computation.2 | async-start | bytes 6291456 | tf_op jit(solution)/shard_map/all_to_all | solution.py:69
  136.7 1.9 copy.34
  138.6 0.0 copy-done
  138.6 0.5 broadcast.195
  139.1 0.7 minimum_reduce_fusion
  139.9 0.1 squeeze.3
  140.0 0.1 min.26
  140.2 70.2 %all-to-all-done.2 = bf16[64,192,128]{2,0,1:T(8,128)(2,1)S(1)} async-done(((bf16[64,192,128]{2,0,1:T(8,128)(2,1)}), bf16[64,192,128]{2,0,1:T(8,128)(2,1)S(1)}, u32[]{:S(2)}, u32[]{:S(2)}) %all-to-all-start.2) | async-done | bytes 3145760 | tf_op jit(solution)/shard_map/all_to_all | solution.py:69
  210.4 2.8 fusion.21
  213.3 0.1 copy.29
  213.3 1.2 gather_fusion.1
  214.5 2.1 select_bitcast_fusion
  216.6 5.4 %all-to-all-start.3 = ((bf16[64,192,128]{2,0,1:T(8,128)(2,1)}), bf16[64,192,128]{2,0,1:T(8,128)(2,1)S(1)}, u32[]{:S(2)}, u32[]{:S(2)}) async-start(bf16[64,192,128]{2,0,1:T(8,128)(2,1)} %select_bitcast_fusion), calls=%async_computation.3 | async-start | bytes 6291456 | tf_op jit(solution)/shard_map/all_to_all | solution.py:81
  222.0 0.2 convert_reduce_fusion.2
  222.2 0.1 select_reduce_fusion
  222.3 1.6 gather_fusion.6
  223.9 0.1 fusion.28
  224.0 0.8 all_to_all.31
  224.8 70.9 %all-to-all-done.3 = bf16[64,192,128]{2,0,1:T(8,128)(2,1)S(1)} async-done(((bf16[64,192,128]{2,0,1:T(8,128)(2,1)}), bf16[64,192,128]{2,0,1:T(8,128)(2,1)S(1)}, u32[]{:S(2)}, u32[]{:S(2)}) %all-to-all-start.3) | async-done | bytes 3145760 | tf_op jit(solution)/shard_map/all_to_all | solution.py:81
  295.8 5.4 %all-to-all-start.5 = ((s32[1,64,3]{2,0,1:T(1,128)}), s32[1,64,3]{2,0,1:T(1,128)S(1)}, u32[]{:S(2)}, u32[]{:S(2)}) async-start(s32[1,64,3]{2,0,1:T(1,128)} %bitcast.12), calls=%async_computation.5 | async-start | bytes 65536 | tf_op jit(solution)/shard_map/all_to_all | solution.py:92
  301.2 2.2 gather_fusion.2
  303.4 4.1 %convolution_bitcast_fusion = bf16[64,128,128]{2,0,1:T(8,128)(2,1)S(1)} fusion(bf16[128,128,128]{2,1,0:T(8,128)(2,1)} %param.10, bf16[128,64,128]{2,1,0:T(8,128)(2,1)} %gather_fusion.2, pred[128]{0:T(512)(128)(4,1)S(1)} %get-tuple-element.11), kind=kOutput, calls=%fused_computation.17 | convolution fusion | flops 269484032 | bytes 8388736 | tf_op jit(solution)/shard_map/mtr,trk->mtk/dot_general | solution.py:83
  307.5 2.7 gather_fusion.5
  310.2 4.3 %fusion = bf16[64,192,128]{2,0,1:T(8,128)(2,1)} fusion(bf16[192,64,128]{2,1,0:T(8,128)(2,1)} %gather_fusion.5, pred[192]{0:T(512)(128)(4,1)S(1)} %get-tuple-element.10, pred[192]{0:T(512)(128)(4,1)S(1)} %fusion.28), kind=kLoop, calls=%fused_computation.9 | loop fusion | flops 3145728 | bytes 6291840 | tf_op jit(solution)/shard_map/convert_element_type | solution.py:90
  314.5 0.0 all-to-all-done.5
  314.5 10.3 %all-to-all-start.4 = ((bf16[64,192,128]{2,0,1:T(8,128)(2,1)}), bf16[64,192,128]{2,0,1:T(8,128)(2,1)S(1)}, u32[]{:S(2)}, u32[]{:S(2)}) async-start(bf16[64,192,128]{2,0,1:T(8,128)(2,1)} %fusion), calls=%async_computation.4 | async-start | bytes 6291456 | tf_op jit(solution)/shard_map/all_to_all | solution.py:89
  324.8 0.6 reduce.12
  325.4 0.1 eq.98
  325.5 73.0 %all-to-all-done.4 = bf16[64,192,128]{2,0,1:T(8,128)(2,1)S(1)} async-done(((bf16[64,192,128]{2,0,1:T(8,128)(2,1)}), bf16[64,192,128]{2,0,1:T(8,128)(2,1)S(1)}, u32[]{:S(2)}, u32[]{:S(2)}) %all-to-all-start.4) | async-done | bytes 3145760 | tf_op jit(solution)/shard_map/all_to_all | solution.py:89
  398.5 1.7 fusion.2
  400.2 0.8 copy.50
  (18 shorter events, 0.1 us)
Async XLA Ops:
  6.5 95.0 %all-gather.2.cloned.1.call-start = ((), (), s32[]{:S(2)}) async-start(), calls=%async_computation.6 | async-start | bytes 8519680 | tf_op jit(solution)/shard_map/all_gather | solution.py:61
  22.2 106.6 %all-to-all-start = ((s32[1,64,3]{2,0,1:T(1,128)}), s32[1,64,3]{2,0,1:T(1,128)S(1)}, u32[]{:S(2)}, u32[]{:S(2)}) async-start(s32[1,64,3]{2,0,1:T(1,128)} %bitcast), calls=%async_computation | async-start | bytes 65536 | tf_op jit(solution)/shard_map/all_to_all | solution.py:72
  128.8 9.8 %copy-start = (s32[2048]{0:T(1024)S(1)}, s32[2048]{0:T(1024)}, u32[]{:S(2)}) copy-start(s32[2048]{0:T(1024)} %param.15) | copy-start | bytes 24580
  128.8 81.6 %all-to-all-start.2 = ((bf16[64,192,128]{2,0,1:T(8,128)(2,1)}), bf16[64,192,128]{2,0,1:T(8,128)(2,1)S(1)}, u32[]{:S(2)}, u32[]{:S(2)}) async-start(bf16[64,192,128]{2,0,1:T(8,128)(2,1)} %fusion.1), calls=%async_computation.2 | async-start | bytes 6291456 | tf_op jit(solution)/shard_map/all_to_all | solution.py:69
  216.6 79.2 %all-to-all-start.3 = ((bf16[64,192,128]{2,0,1:T(8,128)(2,1)}), bf16[64,192,128]{2,0,1:T(8,128)(2,1)S(1)}, u32[]{:S(2)}, u32[]{:S(2)}) async-start(bf16[64,192,128]{2,0,1:T(8,128)(2,1)} %select_bitcast_fusion), calls=%async_computation.3 | async-start | bytes 6291456 | tf_op jit(solution)/shard_map/all_to_all | solution.py:81
  295.8 18.7 %all-to-all-start.5 = ((s32[1,64,3]{2,0,1:T(1,128)}), s32[1,64,3]{2,0,1:T(1,128)S(1)}, u32[]{:S(2)}, u32[]{:S(2)}) async-start(s32[1,64,3]{2,0,1:T(1,128)} %bitcast.12), calls=%async_computation.5 | async-start | bytes 65536 | tf_op jit(solution)/shard_map/all_to_all | solution.py:92
  314.5 84.0 %all-to-all-start.4 = ((bf16[64,192,128]{2,0,1:T(8,128)(2,1)}), bf16[64,192,128]{2,0,1:T(8,128)(2,1)S(1)}, u32[]{:S(2)}, u32[]{:S(2)}) async-start(bf16[64,192,128]{2,0,1:T(8,128)(2,1)} %fusion), calls=%async_computation.4 | async-start | bytes 6291456 | tf_op jit(solution)/shard_map/all_to_all | solution.py:89
Sparse Core Ops, SparseCore 0:
  18.9 82.6 all-gather.1
where the time goes:
time: 409 us; the launch traced here: 408 us
  waiting for transfers between devices  280 us (68%)
  starting transfers between devices  41 us (10%)
  local copies, waits for them, and re-layouts  31.6 us (8%)
  other arithmetic  17.4 us (4%)
  matrix products  14.4 us (4%)
  between operations  13.6 us (3%)
  blocking collectives  9.63 us (2%)
    all_to_all x1, waiting for transfers between devices, body(): lax.all_to_all(sent_back.astype(jnp.bfloat16), 'tile', split_axis=1, conc...  73 us
    all_to_all x1, waiting for transfers between devices, body(): lax.all_to_all(reply_rows, 'tile', split_axis=1, concat_axis=1, tiled=True)  70.9 us
    all_to_all x1, waiting for transfers between devices, body(): lax.all_to_all(sent_terms.astype(jnp.bfloat16), 'tile', split_axis=1, con...  70.2 us
    all_gather x1, waiting for transfers between devices, body(): gathered = lax.all_gather(member_deviations, 'tile', axis=1, tiled=True)  66 us
    all_to_all x1, starting transfers between devices, body(): lax.all_to_all(row_index[None, :], 'tile', split_axis=1, concat_axis=1, t...  12 us
    all_to_all x1, starting transfers between devices, body(): lax.all_to_all(sent_back.astype(jnp.bfloat16), 'tile', split_axis=1, conc...  10.3 us
    all_to_all x1, blocking collectives, sent_to_all(): lax.all_to_all(jnp.broadcast_to(value[None], (size, *value.shape)), axis,...  9.63 us
    reshape x1, local copies, waits for them, and re-layouts, body(): gathered.reshape(local_members, -1, tile_size)  9.01 us
  transfers between devices with their start and end apart: 6, of which 4 were waited for; matrix products, arithmetic and copies ran while one was open for 12% of the time, Pallas kernels for 0%

commit v1 on v0

--- a/solution.py
+++ b/solution.py
@@ -58,7 +58,11 @@
     col_slot = slot_of(col_owner, capacity)
     row_source, row_used = invert(row_slot, slot_total)
     col_source, col_used = invert(col_slot, slot_total)
-    gathered = lax.all_gather(member_deviations, "tile", axis=1, tiled=True)
+    size_2 = lax.axis_size("tile")
+    repeats = [size_2 if d == 1 else 1 for d in range(member_deviations.ndim)]
+    gathered = lax.all_to_all(
+        jnp.tile(member_deviations, repeats), "tile", split_axis=1, concat_axis=1, tiled=True
+    )
     retrieved_blocks = jnp.take(gathered.reshape(local_members, -1, tile_size), tile_col, axis=1)
     forward_terms = jnp.einsum(
         "mtk,trk->mtr", retrieved_blocks, footprints, preferred_element_type=jnp.float32

time: 409 us -> 551 us (1.35)
  waiting for transfers between devices: 280 us -> 396 us
  local copies, waits for them, and re-layouts: 31.6 us -> 63.5 us
  between operations: 13.6 us -> 0.27 us
  starting transfers between devices: 41 us -> 51.3 us
    all_to_all x0 -> x1, waiting for transfers between devices: none -> 182 us  [body(): lax.all_to_all(jnp.tile(member_deviations, repeats), 'tile', split_axis=1...]
    all_gather x1 -> x0, waiting for transfers between devices: 66 us -> none  [body(): gathered = lax.all_gather(member_deviations, 'tile', axis=1, tiled=True)]
    reshape x1 -> x2, local copies, waits for them, and re-layouts: 9.01 us -> 25.3 us  [body(): gathered.reshape(local_members, -1, tile_size)]
    all_to_all x0 -> x1, starting transfers between devices: none -> 12.3 us  [body(): lax.all_to_all(jnp.tile(member_deviations, repeats), 'tile', split_axis=1...]
    all_to_all x0 -> x1, local copies, waits for them, and re-layouts: none -> 11.3 us  [body(): lax.all_to_all(jnp.tile(member_deviations, repeats), 'tile', split_axis=1...]
  transfers between devices with their start and end apart: 6 -> 6, of which waited for: 4 -> 4; matrix products, arithmetic and copies ran while one was open for 12% -> 14% of each run, Pallas kernels for 0% -> 0%
where the time goes in v1:
time: 551 us; the launch traced here: 550 us
  waiting for transfers between devices  396 us (72%)
  local copies, waits for them, and re-layouts  63.5 us (12%)
  starting transfers between devices  51.3 us (9%)
  other arithmetic  14.8 us (3%)
  matrix products  14.4 us (3%)
  blocking collectives  9.63 us (2%)
    all_to_all x1, waiting for transfers between devices, body(): lax.all_to_all(jnp.tile(member_deviations, repeats), 'tile', split_axis=1...  182 us
    all_to_all x1, waiting for transfers between devices, body(): lax.all_to_all(sent_back.astype(jnp.bfloat16), 'tile', split_axis=1, conc...  73 us
    all_to_all x1, waiting for transfers between devices, body(): lax.all_to_all(reply_rows, 'tile', split_axis=1, concat_axis=1, tiled=True)  70.9 us
    all_to_all x1, waiting for transfers between devices, body(): lax.all_to_all(sent_terms.astype(jnp.bfloat16), 'tile', split_axis=1, con...  70.2 us
    reshape x2, local copies, waits for them, and re-layouts, body(): gathered.reshape(local_members, -1, tile_size)  25.3 us
    all_to_all x1, starting transfers between devices, body(): lax.all_to_all(jnp.tile(member_deviations, repeats), 'tile', split_axis=1...  12.3 us
    all_to_all x1, local copies, waits for them, and re-layouts, body(): lax.all_to_all(jnp.tile(member_deviations, repeats), 'tile', split_axis=1...  11.3 us
  transfers between devices with their start and end apart: 6, of which 4 were waited for; matrix products, arithmetic and copies ran while one was open for 14% of the time, Pallas kernels for 0%

profile of v1, /device:TPU:2, one launch (start us, length us, event | category | flops | bytes accessed | tf_op | source)
XLA Modules:
  0.0 550.3 jit_solution(1539384801928295491)
XLA Ops:
  0.0 0.9 convert_reduce_fusion
  1.0 9.6 %all_to_all.45 = f32[4,1,1024]{2,1,0:T(1,128)S(1)} all-to-all(f32[4,1,1024]{2,1,0:T(1,128)S(1)} %broadcast_in_dim.122), channel_id=1, replica_groups=mesh['tile'=64,'mem'=4] {'mem'}, dimensions={0} | all-to-all | bytes 32768 | tf_op jit(solution)/shard_map/all_to_all | solution.py:13
  10.6 0.9 fusion.26
  11.6 4.3 tile.2
  15.8 0.0 copy-start.2
  15.8 0.0 copy-start.1
  15.8 12.3 %all-to-all-start.2 = ((bf16[64,64,1024]{2,0,1:T(8,128)(2,1)}), bf16[64,64,1024]{2,0,1:T(8,128)(2,1)}, u32[]{:S(2)}, u32[]{:S(2)}) async-start(bf16[64,64,1024]{2,0,1:T(8,128)(2,1)} %tile.2), calls=%async_computation.2 | async-start | bytes 16777216 | tf_op jit(solution)/shard_map/all_to_all | solution.py:63
  28.2 0.0 copy-done.2
  28.2 0.2 convert_reduce_fusion.1
  28.4 0.1 select_reduce_fusion.1
  28.5 1.6 gather_fusion.3
  30.1 0.1 fusion.27
  30.2 0.8 all_to_all.29
  31.0 0.0 copy-done.1
  31.0 182.2 %all-to-all-done.2 = bf16[64,64,1024]{2,0,1:T(8,128)(2,1)} async-done(((bf16[64,64,1024]{2,0,1:T(8,128)(2,1)}), bf16[64,64,1024]{2,0,1:T(8,128)(2,1)}, u32[]{:S(2)}, u32[]{:S(2)}) %all-to-all-start.2) | async-done | bytes 8388640 | tf_op jit(solution)/shard_map/all_to_all | solution.py:63
  213.2 7.4 %all-to-all-start = ((s32[1,64,3]{2,0,1:T(1,128)}), s32[1,64,3]{2,0,1:T(1,128)S(1)}, u32[]{:S(2)}, u32[]{:S(2)}) async-start(s32[1,64,3]{2,0,1:T(1,128)} %bitcast), calls=%async_computation | async-start | bytes 65536 | tf_op jit(solution)/shard_map/all_to_all | solution.py:76
  220.6 11.3 %copy.29 = bf16[64,64,1024]{2,1,0:T(8,128)(2,1)} copy(bf16[64,64,1024]{2,0,1:T(8,128)(2,1)} %all-to-all-done.2) | data formatting | bytes 16777216 | tf_op jit(solution)/shard_map/all_to_all | solution.py:63
  231.9 13.3 %reshape.92 = bf16[64,512,128]{2,1,0:T(8,128)(2,1)} reshape(bf16[64,64,1024]{2,1,0:T(8,128)(2,1)} %copy.29) | data formatting | bytes 16777216 | tf_op jit(solution)/shard_map/reshape | solution.py:66
  245.2 12.0 %copy.30 = bf16[64,512,128]{2,0,1:T(8,128)(2,1)} copy(bf16[64,512,128]{2,1,0:T(8,128)(2,1)} %reshape.92) | data formatting | bytes 16777216 | tf_op jit(solution)/shard_map/reshape | solution.py:66
  257.2 5.5 %gather_fusion = bf16[128,64,128]{2,1,0:T(8,128)(2,1)} fusion(bf16[64,512,128]{2,0,1:T(8,128)(2,1)} %copy.30, s32[1024]{0:T(1024)S(1)} %pad_clamp_fusion.3), kind=kCustom, calls=%fused_computation.4 | custom fusion | bytes 4194816 | tf_op jit(solution)/shard_map/jit(_take)/gather | solution.py:66
  262.8 5.8 %convolution_bitcast_fusion.1 = bf16[64,128,128]{2,0,1:T(8,128)(2,1)S(1)} fusion(bf16[128,128,128]{2,1,0:T(8,128)(2,1)} %param.10, bf16[128,64,128]{2,1,0:T(8,128)(2,1)} %gather_fusion, pred[128]{0:T(512)(128)(4,1)S(1)} %compare_and_fusion.2), kind=kOutput, calls=%fused_computation.17 | convolution fusion | flops 269484032 | bytes 8388736 | tf_op jit(solution)/shard_map/mtk,trk->mtr/dot_general | solution.py:67
  268.5 2.7 gather_fusion.4
  271.2 4.3 fusion.1
  275.5 0.0 copy-start
  275.5 0.0 all-to-all-done
  275.5 10.4 %all-to-all-start.3 = ((bf16[64,192,128]{2,0,1:T(8,128)(2,1)}), bf16[64,192,128]{2,0,1:T(8,128)(2,1)S(1)}, u32[]{:S(2)}, u32[]{:S(2)}) async-start(bf16[64,192,128]{2,0,1:T(8,128)(2,1)} %fusion.1), calls=%async_computation.3 | async-start | bytes 6291456 | tf_op jit(solution)/shard_map/all_to_all | solution.py:73
  286.0 1.9 copy.36
  287.9 0.0 copy-done
  287.9 0.5 broadcast.198
  288.4 0.7 minimum_reduce_fusion
  289.1 0.1 squeeze.3
  289.3 0.1 min.26
  289.5 70.2 %all-to-all-done.3 = bf16[64,192,128]{2,0,1:T(8,128)(2,1)S(1)} async-done(((bf16[64,192,128]{2,0,1:T(8,128)(2,1)}), bf16[64,192,128]{2,0,1:T(8,128)(2,1)S(1)}, u32[]{:S(2)}, u32[]{:S(2)}) %all-to-all-start.3) | async-done | bytes 3145760 | tf_op jit(solution)/shard_map/all_to_all | solution.py:73
  359.7 2.8 fusion.21
  362.5 0.1 copy.32
  362.6 1.2 gather_fusion.1
  363.8 2.1 select_bitcast_fusion
  365.8 5.4 all-to-all-start.4
  371.3 0.2 convert_reduce_fusion.2
  371.5 0.1 select_reduce_fusion
  371.6 1.6 gather_fusion.6
  373.2 0.1 fusion.28
  373.3 0.8 all_to_all.36
  374.1 70.9 %all-to-all-done.4 = bf16[64,192,128]{2,0,1:T(8,128)(2,1)S(1)} async-done(((bf16[64,192,128]{2,0,1:T(8,128)(2,1)}), bf16[64,192,128]{2,0,1:T(8,128)(2,1)S(1)}, u32[]{:S(2)}, u32[]{:S(2)}) %all-to-all-start.4) | async-done | bytes 3145760 | tf_op jit(solution)/shard_map/all_to_all | solution.py:85
  445.0 5.4 all-to-all-start.6
  450.5 2.2 gather_fusion.2
  452.6 4.1 convolution_bitcast_fusion
  456.7 2.7 gather_fusion.5
  459.5 4.3 fusion
  463.7 0.0 all-to-all-done.6
  463.7 10.3 %all-to-all-start.5 = ((bf16[64,192,128]{2,0,1:T(8,128)(2,1)}), bf16[64,192,128]{2,0,1:T(8,128)(2,1)S(1)}, u32[]{:S(2)}, u32[]{:S(2)}) async-start(bf16[64,192,128]{2,0,1:T(8,128)(2,1)} %fusion), calls=%async_computation.5 | async-start | bytes 6291456 | tf_op jit(solution)/shard_map/all_to_all | solution.py:93
  474.0 0.6 reduce.12
  474.7 0.1 eq.98
  474.8 73.0 %all-to-all-done.5 = bf16[64,192,128]{2,0,1:T(8,128)(2,1)S(1)} async-done(((bf16[64,192,128]{2,0,1:T(8,128)(2,1)}), bf16[64,192,128]{2,0,1:T(8,128)(2,1)S(1)}, u32[]{:S(2)}, u32[]{:S(2)}) %all-to-all-start.5) | async-done | bytes 3145760 | tf_op jit(solution)/shard_map/all_to_all | solution.py:93
  547.8 1.7 fusion.2
  549.5 0.8 copy.51
  (21 shorter events, 0.2 us)
Async XLA Ops:
  15.8 12.4 %copy-start.2 = (s32[128]{0:T(128)S(1)}, s32[128]{0:T(128)}, u32[]{:S(2)}) copy-start(s32[128]{0:T(128)} %param.11) | copy-start | bytes 1540
  15.8 15.2 %copy-start.1 = (s32[128]{0:T(128)S(1)}, s32[128]{0:T(128)}, u32[]{:S(2)}) copy-start(s32[128]{0:T(128)} %param.12) | copy-start | bytes 1540
  15.8 197.4 %all-to-all-start.2 = ((bf16[64,64,1024]{2,0,1:T(8,128)(2,1)}), bf16[64,64,1024]{2,0,1:T(8,128)(2,1)}, u32[]{:S(2)}, u32[]{:S(2)}) async-start(bf16[64,64,1024]{2,0,1:T(8,128)(2,1)} %tile.2), calls=%async_computation.2 | async-start | bytes 16777216 | tf_op jit(solution)/shard_map/all_to_all | solution.py:63
  213.2 62.3 %all-to-all-start = ((s32[1,64,3]{2,0,1:T(1,128)}), s32[1,64,3]{2,0,1:T(1,128)S(1)}, u32[]{:S(2)}, u32[]{:S(2)}) async-start(s32[1,64,3]{2,0,1:T(1,128)} %bitcast), calls=%async_computation | async-start | bytes 65536 | tf_op jit(solution)/shard_map/all_to_all | solution.py:76
  275.5 12.4 %copy-start = (s32[2048]{0:T(1024)S(1)}, s32[2048]{0:T(1024)}, u32[]{:S(2)}) copy-start(s32[2048]{0:T(1024)} %param.15) | copy-start | bytes 24580
  275.5 84.2 %all-to-all-start.3 = ((bf16[64,192,128]{2,0,1:T(8,128)(2,1)}), bf16[64,192,128]{2,0,1:T(8,128)(2,1)S(1)}, u32[]{:S(2)}, u32[]{:S(2)}) async-start(bf16[64,192,128]{2,0,1:T(8,128)(2,1)} %fusion.1), calls=%async_computation.3 | async-start | bytes 6291456 | tf_op jit(solution)/shard_map/all_to_all | solution.py:73
  365.8 79.2 %all-to-all-start.4 = ((bf16[64,192,128]{2,0,1:T(8,128)(2,1)}), bf16[64,192,128]{2,0,1:T(8,128)(2,1)S(1)}, u32[]{:S(2)}, u32[]{:S(2)}) async-start(bf16[64,192,128]{2,0,1:T(8,128)(2,1)} %select_bitcast_fusion), calls=%async_computation.4 | async-start | bytes 6291456 | tf_op jit(solution)/shard_map/all_to_all | solution.py:85
  445.0 18.7 %all-to-all-start.6 = ((s32[1,64,3]{2,0,1:T(1,128)}), s32[1,64,3]{2,0,1:T(1,128)S(1)}, u32[]{:S(2)}, u32[]{:S(2)}) async-start(s32[1,64,3]{2,0,1:T(1,128)} %bitcast.12), calls=%async_computation.6 | async-start | bytes 65536 | tf_op jit(solution)/shard_map/all_to_all | solution.py:96
  463.7 84.0 %all-to-all-start.5 = ((bf16[64,192,128]{2,0,1:T(8,128)(2,1)}), bf16[64,192,128]{2,0,1:T(8,128)(2,1)S(1)}, u32[]{:S(2)}, u32[]{:S(2)}) async-start(bf16[64,192,128]{2,0,1:T(8,128)(2,1)} %fusion), calls=%async_computation.5 | async-start | bytes 6291456 | tf_op jit(solution)/shard_map/all_to_all | solution.py:93
